TPU v7x, 32 devices: a whole 2x2x4 slice. The times are simulated.
32 devices in a mesh: scene: 4 (over x, core), seq: 8 (over z, y).
Axes of the slice: x: 2, y: 2, z: 4, core: 2. Of those that a mesh axis runs over, the one named last changes fastest.
Arguments:
- tokens: bfloat16 [10240, 768], P(('scene', 'seq')), may hold values from -6 to 6
- scene_tokens: int32 [4], P('scene'), may hold values from 128 to 320, as said below
- cotangent: bfloat16 [10240, 768], P(('scene', 'seq')), may hold values from -6 to 6
- qkv_master: float32 [768, 2304], P(('scene', 'seq')), may hold values from -0.21875 to 0.21875
- out_master: float32 [768, 768], P(('scene', 'seq')), may hold values from -6 to 6
- up_master: float32 [768, 3072], P(('scene', 'seq')), may hold values from -0.21875 to 0.21875
- down_master: float32 [3072, 768], P(('scene', 'seq')), may hold values from -0.109375 to 0.109375
- gain_one: float32 [768], replicated, may hold values from 0.5 to 1.5
- gain_two: float32 [768], replicated, may hold values from 0.5 to 1.5
Outputs:
- mixed: bfloat16 [10240, 768], P(('scene', 'seq'))
- input_grad: float32 [10240, 768], P(('scene', 'seq'))
- qkv_grad: float32 [768, 2304], P(('scene', 'seq'))
- out_grad: float32 [768, 768], P(('scene', 'seq'))
- up_grad: float32 [768, 3072], P(('scene', 'seq'))
- down_grad: float32 [3072, 768], P(('scene', 'seq'))
- gain_one_grad: float32 [768], P(('scene', 'seq'))
- gain_two_grad: float32 [768], P(('scene', 'seq'))
Inputs may be any that keep to these rules, and one draw needn't show every extreme that they name: Slots 0 to scene_tokens[s] - 1 of every device of scene s's group hold that scene's tokens, the others are padding; one scene, drawn from the seed, has all 320 slots of every device live.
All inputs are finite; a program needn't handle non-finite values.
Results may differ from a plain program's by a relative error of at most 0.02.
Values may be sent and summed in bfloat16 or wider, within the bound.
No kernel may reach another device: no remote copies, remote signals or barrier semaphores. Data moves between devices by JAX's collectives and lax.ppermute only.
A program may use at most 512 MiB of HBM per device.

v0:
```python
import jax
import jax.numpy as jnp
from jax import lax
from jax.sharding import PartitionSpec as P

HEADS = 12
HEAD = 64
NEG_BIG = -1e30


def norm_rows(values, gain_vector):
    mean_value = jnp.mean(values, axis=-1, keepdims=True)
    centered = values - mean_value
    variance = jnp.mean(centered * centered, axis=-1, keepdims=True)
    inverse = lax.rsqrt(variance + 1e-05)
    scaled = centered * inverse
    return (scaled * gain_vector, scaled, inverse)


def norm_back(grad_result, scaled, inverse, gain_vector):
    grad_scaled = grad_result * gain_vector
    first_mean = jnp.mean(grad_scaled, axis=-1, keepdims=True)
    second_mean = jnp.mean(grad_scaled * scaled, axis=-1, keepdims=True)
    grad_input = inverse * (grad_scaled - first_mean - scaled * second_mean)
    return (grad_input, jnp.sum(grad_result * scaled, axis=0))


def split_heads(values):
    return values.reshape(values.shape[0], HEADS, HEAD)


def score_grads(query_part, grad_part, key_part, value_part, lse_part, delta_part, live_keys):
    scores = (
        jnp.einsum("qhd,khd->hqk", query_part, key_part, preferred_element_type=jnp.float32) * 0.125
    )
    weights_now = jnp.where(live_keys[None, None, :], jnp.exp(scores - lse_part[:, :, None]), 0.0)
    grad_weights = jnp.einsum(
        "qhd,khd->hqk", grad_part, value_part, preferred_element_type=jnp.float32
    )
    dscore = (weights_now * (grad_weights - delta_part[:, :, None])).astype(jnp.bfloat16)
    return (weights_now.astype(jnp.bfloat16), dscore)


def on_device(
    tokens,
    scene_tokens,
    cotangent,
    qkv_master,
    out_master,
    up_master,
    down_master,
    gain_one,
    gain_two,
):
    local_rows = tokens.shape[0]
    model_width = tokens.shape[1]
    live_count = scene_tokens[0]
    local_live = jnp.arange(local_rows, dtype=jnp.int32) < live_count
    qkv_part = qkv_master.astype(jnp.bfloat16)
    out_part = out_master.astype(jnp.bfloat16)
    up_part = up_master.astype(jnp.bfloat16)
    down_part = down_master.astype(jnp.bfloat16)
    qkv_weight, out_weight, up_weight, down_weight = (
        lax.all_gather(qkv_part, ("scene", "seq"), axis=0, tiled=True),
        lax.all_gather(out_part, ("scene", "seq"), axis=0, tiled=True),
        lax.all_gather(up_part, ("scene", "seq"), axis=0, tiled=True),
        lax.all_gather(down_part, ("scene", "seq"), axis=0, tiled=True),
    )
    inputs = tokens.astype(jnp.float32)
    normed_one, scaled_one, inverse_one = norm_rows(inputs, gain_one)
    normed_low = normed_one.astype(jnp.bfloat16)
    qkv_rows = jnp.dot(normed_low, qkv_weight, preferred_element_type=jnp.float32).astype(
        jnp.bfloat16
    )
    queries = qkv_rows[:, :model_width]
    key_rows = qkv_rows[:, model_width : 2 * model_width]
    value_rows = qkv_rows[:, 2 * model_width :]
    query_heads = split_heads(queries)

    def piece_live(piece_rows):
        places = jnp.arange(piece_rows, dtype=jnp.int32)
        return places % local_rows < live_count

    row_max = jnp.full((HEADS, local_rows), NEG_BIG, jnp.float32)
    key_piece = lax.all_gather(key_rows, "seq", axis=0, tiled=True)
    value_piece = lax.all_gather(value_rows, "seq", axis=0, tiled=True)
    piece_rows = key_piece.shape[0]
    scores = (
        jnp.einsum(
            "qhd,khd->hqk", query_heads, split_heads(key_piece), preferred_element_type=jnp.float32
        )
        * 0.125
    )
    scores = jnp.where(piece_live(piece_rows)[None, None, :], scores, NEG_BIG)
    new_max = jnp.maximum(row_max, jnp.max(scores, axis=-1))
    exponent = jnp.exp(scores - new_max[:, :, None])
    new_sum = jnp.sum(exponent, axis=-1)
    update = jnp.einsum(
        "hqk,khd->hqd",
        exponent.astype(jnp.bfloat16),
        split_heads(value_piece),
        preferred_element_type=jnp.float32,
    )
    row_lse = new_max + jnp.log(new_sum)
    attended = (
        (update / new_sum[:, :, None])
        .transpose(1, 0, 2)
        .reshape(local_rows, model_width)
        .astype(jnp.bfloat16)
    )
    resid = inputs + jnp.dot(attended, out_weight, preferred_element_type=jnp.float32)
    normed_two, scaled_two, inverse_two = norm_rows(resid, gain_two)
    normed_two_low = normed_two.astype(jnp.bfloat16)
    upper = jnp.dot(normed_two_low, up_weight, preferred_element_type=jnp.float32)
    activated, gelu_back = jax.vjp(jax.nn.gelu, upper)
    activated_low = activated.astype(jnp.bfloat16)
    mixed = (
        resid + jnp.dot(activated_low, down_weight, preferred_element_type=jnp.float32)
    ).astype(jnp.bfloat16)
    grad_result = cotangent.astype(jnp.float32) * local_live[:, None].astype(jnp.float32)
    grad_low = grad_result.astype(jnp.bfloat16)
    down_grad = jnp.einsum("tf,td->fd", activated_low, grad_low, preferred_element_type=jnp.float32)
    grad_active = jnp.einsum("td,fd->tf", grad_low, down_weight, preferred_element_type=jnp.float32)
    grad_upper = gelu_back(grad_active)[0].astype(jnp.bfloat16)
    up_grad = jnp.einsum(
        "td,tf->df", normed_two_low, grad_upper, preferred_element_type=jnp.float32
    )
    grad_normed_two = jnp.einsum(
        "tf,df->td", grad_upper, up_weight, preferred_element_type=jnp.float32
    )
    grad_norm_second, gain_two_grad = norm_back(grad_normed_two, scaled_two, inverse_two, gain_two)
    grad_resid = grad_result + grad_norm_second
    grad_branch = grad_resid.astype(jnp.bfloat16)
    out_grad = jnp.einsum("te,td->ed", attended, grad_branch, preferred_element_type=jnp.float32)
    grad_attended = jnp.einsum(
        "td,ed->te", grad_branch, out_weight, preferred_element_type=jnp.float32
    ).astype(jnp.bfloat16)
    grad_heads = split_heads(grad_attended)
    delta = jnp.sum(
        grad_heads.astype(jnp.float32) * split_heads(attended).astype(jnp.float32), axis=-1
    ).T
    total_rows = local_rows * lax.axis_size("seq")
    key_piece = lax.all_gather(key_rows, "seq", axis=0, tiled=True)
    value_piece = lax.all_gather(value_rows, "seq", axis=0, tiled=True)
    piece_rows = key_piece.shape[0]
    key_heads = split_heads(key_piece)
    weights_low, dscore = score_grads(
        query_heads,
        grad_heads,
        key_heads,
        split_heads(value_piece),
        row_lse,
        delta,
        piece_live(piece_rows),
    )
    grad_query = (
        jnp.einsum("hqk,khd->qhd", dscore, key_heads, preferred_element_type=jnp.float32) * 0.125
    )
    key_terms = (
        jnp.einsum("hqk,qhd->khd", dscore, query_heads, preferred_element_type=jnp.float32) * 0.125
    )
    value_terms = jnp.einsum(
        "hqk,qhd->khd", weights_low, grad_heads, preferred_element_type=jnp.float32
    )
    key_buffer = key_terms
    value_buffer = value_terms
    grad_query, key_buffer, value_buffer = (grad_query, key_buffer, value_buffer)
    grad_keys, grad_values = (
        lax.psum_scatter(
            key_buffer.reshape(total_rows, model_width).astype(jnp.bfloat16),
            "seq",
            scatter_dimension=0,
            tiled=True,
        ).astype(jnp.float32),
        lax.psum_scatter(
            value_buffer.reshape(total_rows, model_width).astype(jnp.bfloat16),
            "seq",
            scatter_dimension=0,
            tiled=True,
        ).astype(jnp.float32),
    )
    grad_qkv = jnp.concatenate(
        [grad_query.reshape(local_rows, model_width), grad_keys, grad_values], axis=1
    ).astype(jnp.bfloat16)
    qkv_grad = jnp.einsum("td,te->de", normed_low, grad_qkv, preferred_element_type=jnp.float32)
    grad_normed_one = jnp.einsum(
        "te,de->td", grad_qkv, qkv_weight, preferred_element_type=jnp.float32
    )
    grad_norm_first, gain_one_grad = norm_back(grad_normed_one, scaled_one, inverse_one, gain_one)
    input_grad = grad_resid + grad_norm_first
    qkv_share, out_share, up_share, down_share, first_share, second_share = (
        lax.psum_scatter(qkv_grad, ("scene", "seq"), scatter_dimension=0, tiled=True),
        lax.psum_scatter(out_grad, ("scene", "seq"), scatter_dimension=0, tiled=True),
        lax.psum_scatter(up_grad, ("scene", "seq"), scatter_dimension=0, tiled=True),
        lax.psum_scatter(down_grad, ("scene", "seq"), scatter_dimension=0, tiled=True),
        lax.psum_scatter(gain_one_grad, ("scene", "seq"), scatter_dimension=0, tiled=True),
        lax.psum_scatter(gain_two_grad, ("scene", "seq"), scatter_dimension=0, tiled=True),
    )
    return (
        mixed,
        input_grad,
        qkv_share,
        out_share,
        up_share,
        down_share,
        first_share,
        second_share,
    )


def solution(mesh):
    in_specs = (
        P(("scene", "seq"), None),
        P("scene"),
        P(("scene", "seq"), None),
        P(("scene", "seq"), None),
        P(("scene", "seq"), None),
        P(("scene", "seq"), None),
        P(("scene", "seq"), None),
        P(),
        P(),
    )
    out_specs = (
        P(("scene", "seq"), None),
        P(("scene", "seq"), None),
        P(("scene", "seq"), None),
        P(("scene", "seq"), None),
        P(("scene", "seq"), None),
        P(("scene", "seq"), None),
        P(("scene", "seq")),
        P(("scene", "seq")),
    )
    return jax.shard_map(
        on_device, mesh=mesh, in_specs=in_specs, out_specs=out_specs, check_vma=False
    )
```

profile of v0, /device:TPU:0, one launch (start us, length us, event | category | flops | bytes accessed | tf_op | source)
XLA Modules:
  0.0 1135.8 jit_solution(7848209360860348284)
XLA Ops:
  7.2 1.6 convert_element_type.98
  8.8 0.0 all-gather.9.cloned.1.call-start
  8.9 1.2 convert_reduce_fusion
  10.1 1.3 fusion.36
  11.4 63.0 %all-gather.7.cloned.1.call-done = bf16[768,2304]{1,0:T(8,128)(2,1)} async-done(((bf16[24,2304]{1,0:T(8,128)(2,1)}), bf16[768,2304]{1,0:T(8,128)(2,1)}) %all-gather.7.cloned.1.call-update) | async-done | bytes 3538960 | tf_op jit(solution)/shard_map/all_gather | solution.py:64
  74.4 3.6 convolution_convert_fusion
  78.0 1.0 fusion.66
  79.1 0.7 all-gather.11.cloned.1.call-update
  79.9 0.6 convert_element_type.103
  80.6 0.7 convert_element_type.105
  81.3 0.0 all-gather.17.cloned.1.call-start
  81.3 0.7 convert_element_type.107
  82.0 0.0 reduce-scatter.21.cloned.1.call-start
  82.8 0.3 copy.28
  83.1 65.0 %all-gather.9.cloned.1.call-done = bf16[2560,768]{1,0:T(8,128)(2,1)} async-done(((bf16[320,768]{1,0:T(8,128)(2,1)}), bf16[2560,768]{1,0:T(8,128)(2,1)}) %all-gather.9.cloned.1.call-update) | async-done | bytes 3932176 | tf_op jit(solution)/shard_map/all_gather | solution.py:85
  148.1 6.3 copy.29
  154.4 17.1 %select_reduce_fusion = (f32[12,320]{1,0:T(8,128)S(1)}, f32[12,320,2560]{2,1,0:T(8,128)}) fusion(pred[2560]{0:T(1024)(128)(4,1)S(1)} %fusion.51, bf16[320,12,64]{0,2,1:T(8,128)(2,1)S(1)} %bitcast.50, bf16[2560,12,64]{0,2,1:T(8,128)(2,1)} %bitcast.47), kind=kOutput, calls=%fused_computation.3 | convolution fusion | flops 1287778560 | bytes 43763200 | tf_op jit(solution)/shard_map/qhd,khd->hqk/dot_general | solution.py:89
  171.5 47.9 %all-gather.11.cloned.1.call-done = bf16[2560,768]{1,0:T(8,128)(2,1)} async-done(((bf16[320,768]{1,0:T(8,128)(2,1)}), bf16[2560,768]{1,0:T(8,128)(2,1)}) %all-gather.11.cloned.1.call-update) | async-done | bytes 3932176 | tf_op jit(solution)/shard_map/all_gather | solution.py:86
  219.4 6.2 copy.30
  225.6 18.1 %fusion = f32[12,320]{1,0:T(8,128)S(1)} fusion(f32[12,320,2560]{2,1,0:T(8,128)} %get-tuple-element.20, f32[12,320]{1,0:T(8,128)S(1)} %broadcast_maximum_fusion, pred[2560]{0:T(1024)(128)(4,1)S(1)} %fusion.51), kind=kLoop, calls=%fused_computation.4 | loop fusion | flops 39317760 | bytes 39354880 | tf_op jit(solution)/shard_map/reduce_sum | solution.py:97
  243.8 15.2 %divide_convert_fusion = bf16[320,12,64]{0,2,1:T(8,128)(2,1)S(1)} fusion(bf16[2560,12,64]{0,2,1:T(8,128)(2,1)S(1)} %bitcast.55, f32[12,320,2560]{2,1,0:T(8,128)} %get-tuple-element.20, f32[12,320]{1,0:T(8,128)S(1)} %broadcast_maximum_fusion, pred[2560]{0:T(1024)(128)(4,1)S(1)} %fusion.51, f32[320,12]{0,1:T(8,128)S(1)} %bitcast.62), kind=kOutput, calls=%fused_computation.35 | convolution fusion | flops 1298104320 | bytes 43778560 | tf_op jit(solution)/shard_map/hqk,khd->hqd/dot_general | solution.py:98
  259.0 16.4 %all-gather.13.cloned.1.call-done = bf16[768,768]{1,0:T(8,128)(2,1)} async-done(((bf16[24,768]{1,0:T(8,128)(2,1)}), bf16[768,768]{1,0:T(8,128)(2,1)}) %all-gather.13.cloned.1.call-update) | async-done | bytes 1179664 | tf_op jit(solution)/shard_map/all_gather | solution.py:65
  275.4 1.9 fusion.67
  277.3 0.3 multiply_reduce_fusion.3
  277.6 0.6 log_add_fusion
  278.2 63.0 %all-gather.15.cloned.1.call-done = bf16[768,3072]{1,0:T(8,128)(2,1)} async-done(((bf16[24,3072]{1,0:T(8,128)(2,1)}), bf16[768,3072]{1,0:T(8,128)(2,1)}) %all-gather.15.cloned.1.call-update) | async-done | bytes 4718608 | tf_op jit(solution)/shard_map/all_gather | solution.py:66
  341.3 6.0 fusion.65
  347.3 59.8 %all-gather.17.cloned.1.call-done = bf16[3072,768]{1,0:T(8,128)(2,1)} async-done(((bf16[96,768]{1,0:T(8,128)(2,1)}), bf16[3072,768]{1,0:T(8,128)(2,1)}) %all-gather.17.cloned.1.call-update) | async-done | bytes 4718608 | tf_op jit(solution)/shard_map/all_gather | solution.py:67
  407.1 7.8 fusion.18
  415.0 2.5 multiply_reduce_fusion.1
  417.5 0.4 multiply_add_fusion
  417.9 0.6 convolution_convert_fusion.1
  418.5 1.1 copy.31
  419.5 18.2 %fusion.9 = bf16[12,64,2560]{2,1,0:T(8,128)(2,1)} fusion(bf16[320,12,64]{0,2,1:T(8,128)(2,1)} %bitcast.59, f32[12,320,2560]{2,1,0:T(8,128)} %get-tuple-element.20, f32[12,320]{1,0:T(8,128)} %log_add_fusion, pred[2560]{0:T(1024)(128)(4,1)S(1)} %fusion.51), kind=kOutput, calls=%fused_computation.14 | convolution fusion | flops 1299578880 | bytes 43763200 | tf_op jit(solution)/shard_map/hqk,qhd->khd/dot_general | solution.py:162
  437.7 6.3 copy.34
  444.1 0.0 reduce-scatter.19.cloned.1.call-start
  444.1 1.4 multiply_reduce_fusion
  445.6 26.5 %multiply_convert_fusion = bf16[12,320,2560]{2,1,0:T(8,128)(2,1)} fusion(f32[12,320,2560]{2,1,0:T(8,128)} %get-tuple-element.20, bf16[320,12,64]{0,2,1:T(8,128)(2,1)} %bitcast.61, bf16[2560,12,64]{0,2,1:T(8,128)(2,1)} %bitcast.54, f32[12,320]{1,0:T(8,128)S(1)} %bitcast.63, f32[12,320]{1,0:T(8,128)S(1)} %copy-done.19, pred[2560]{0:T(1024)(128)(4,1)S(1)} %fusion.51), kind=kOutput, calls=%fused_computation | convolution fusion | flops 1317273600 | bytes 63439360 | tf_op jit(solution)/shard_map/qhd,khd->hqk/dot_general | solution.py:37
  472.1 12.6 %multiply_convert_fusion.1 = bf16[12,64,2560]{2,1,0:T(8,128)(2,1)} fusion(bf16[320,12,64]{0,2,1:T(8,128)(2,1)S(1)} %bitcast.51, bf16[12,320,2560]{2,1,0:T(8,128)(2,1)} %multiply_convert_fusion), kind=kOutput, calls=%fused_computation.11 | convolution fusion | flops 1262223360 | bytes 24084480 | tf_op jit(solution)/shard_map/hqk,qhd->khd/dot_general | solution.py:160
  484.7 6.3 copy.32
  491.0 0.0 reduce-scatter.13.cloned.1.call-start
  491.1 1.0 copy-done.2
  492.1 2.2 fusion.42
  494.3 0.0 reduce-scatter.15.cloned.1.call-start
  494.3 6.8 fusion.64
  501.2 0.0 reduce-scatter.17.cloned.1.call-start
  501.2 1.0 copy-done.9
  502.2 8.7 fusion.45
  511.0 10.9 fusion.23
  522.0 5.4 reduce-scatter.21.cloned.1.call-done
  527.4 2.1 copy.35
  529.5 86.1 %reduce-scatter.19.cloned.1.call-done = bf16[320,768]{1,0:T(8,128)(2,1)} async-done(((bf16[2560,768]{1,0:T(8,128)(2,1)}), bf16[320,768]{1,0:T(8,128)(2,1)}) %reduce-scatter.19.cloned.1.call-update) | async-done | bytes 491536
  615.6 2.1 copy.33
  617.7 6.4 fusion.38
  624.1 6.9 fusion.22
  631.0 1.9 fusion.35
  632.9 40.4 %all-reduce.2 = (f32[768]{0:T(1024)S(1)}, f32[768]{0:T(1024)S(1)}) all-reduce(f32[768]{0:T(1024)S(1)} %get-tuple-element.10, f32[768]{0:T(1024)S(1)} %copy-done.23), channel_id=8, replica_groups=mesh['scene'=4,'seq'=8] {'scene','seq'}, use_global_device_ids=true, to_apply=%region_18.19.clone | all-reduce | flops 1536 | bytes 12288
  673.4 0.6 dynamic-slice
  673.9 0.6 dynamic-slice.1
  674.5 1.3 fusion.34
  675.8 44.5 %reduce-scatter.13.cloned.1.call-done = f32[24,768]{1,0:T(8,128)} async-done(((f32[768,768]{1,0:T(8,128)}), f32[24,768]{1,0:T(8,128)}) %reduce-scatter.13.cloned.1.call-update) | async-done | bytes 73744 | tf_op jit(solution)/shard_map/reduce_scatter | solution.py:193
  720.3 142.0 %reduce-scatter.15.cloned.1.call-done = f32[24,3072]{1,0:T(8,128)} async-done(((f32[768,3072]{1,0:T(8,128)}), f32[24,3072]{1,0:T(8,128)}) %reduce-scatter.15.cloned.1.call-update) | async-done | bytes 294928 | tf_op jit(solution)/shard_map/reduce_scatter | solution.py:194
  862.3 141.0 %reduce-scatter.17.cloned.1.call-done = f32[96,768]{1,0:T(8,128)} async-done(((f32[3072,768]{1,0:T(8,128)}), f32[96,768]{1,0:T(8,128)}) %reduce-scatter.17.cloned.1.call-update) | async-done | bytes 294928 | tf_op jit(solution)/shard_map/reduce_scatter | solution.py:195
  1003.3 125.4 %reduce-scatter.11.cloned.1.call-done = f32[24,2304]{1,0:T(8,128)} async-done(((f32[768,2304]{1,0:T(8,128)}), f32[24,2304]{1,0:T(8,128)}) %reduce-scatter.11.cloned.1.call-update) | async-done | bytes 221200 | tf_op jit(solution)/shard_map/reduce_scatter | solution.py:192
  (76 shorter events, 0.6 us)
Async XLA Ops:
  7.2 67.2 %all-gather.7.cloned.1.call-start = ((), (), s32[]{:S(2)}) async-start(), calls=%async_computation.6 | async-start | bytes 3649536 | tf_op jit(solution)/shard_map/all_gather | solution.py:64
  8.8 139.3 %all-gather.9.cloned.1.call-start = ((), (), s32[]{:S(2)}) async-start(), calls=%async_computation.7 | async-start | bytes 4423680 | tf_op jit(solution)/shard_map/all_gather | solution.py:85
  10.1 64.3 %copy-start.15 = (f32[320]{0:T(512)}, f32[320]{0:T(512)S(1)}, u32[]{:S(2)}) copy-start(f32[320]{0:T(512)S(1)} %broadcast_multiply_fusion.5) | copy-start | bytes 3844
  11.4 63.0 %copy-start.17 = (f32[320]{0:T(512)}, f32[320]{0:T(512)S(1)}, u32[]{:S(2)}) copy-start(f32[320]{0:T(512)S(1)} %add_rsqrt_fusion.1) | copy-start | bytes 3844
  78.0 1.9 copy-start.14
  78.0 2.6 copy-start.10
  78.0 3.3 copy-start.11
  79.1 140.3 %all-gather.11.cloned.1.call-start = ((), (), s32[]{:S(2)}) async-start(), calls=%async_computation.8 | async-start | bytes 4423680 | tf_op jit(solution)/shard_map/all_gather | solution.py:86
  79.8 195.6 %all-gather.13.cloned.1.call-start = ((), (), s32[]{:S(2)}) async-start(), calls=%async_computation.9 | async-start | bytes 1216512 | tf_op jit(solution)/shard_map/all_gather | solution.py:65
  80.5 260.8 %all-gather.15.cloned.1.call-start = ((), (), s32[]{:S(2)}) async-start(), calls=%async_computation.10 | async-start | bytes 4866048 | tf_op jit(solution)/shard_map/all_gather | solution.py:66
  81.3 325.8 %all-gather.17.cloned.1.call-start = ((), (), s32[]{:S(2)}) async-start(), calls=%async_computation.11 | async-start | bytes 4866048 | tf_op jit(solution)/shard_map/all_gather | solution.py:67
  82.0 445.4 %reduce-scatter.21.cloned.1.call-start = ((), (), s32[]{:S(2)}) async-start(), calls=%async_computation.17 | async-start | bytes 4423680
  82.8 324.4 %copy-start.20 = (f32[320]{0:T(512)}, f32[320]{0:T(512)S(1)}, u32[]{:S(2)}) copy-start(f32[320]{0:T(512)S(1)} %fusion.55) | copy-start | bytes 3844
  225.6 18.1 %copy-start.4 = (bf16[2560,768]{0,1:T(8,128)(2,1)S(1)}, bf16[2560,768]{0,1:T(8,128)(2,1)}, u32[]{:S(2)}) copy-start(bf16[2560,768]{0,1:T(8,128)(2,1)} %copy.30) | copy-start | bytes 11796484
  243.7 31.6 %copy-start = (bf16[320,768]{1,0:T(8,128)(2,1)S(1)}, bf16[320,768]{1,0:T(8,128)(2,1)}, u32[]{:S(2)}) copy-start(bf16[320,768]{1,0:T(8,128)(2,1)} %param.9) | copy-start | bytes 1474564
  259.0 88.3 %copy-start.1 = (bf16[320,12,64]{0,2,1:T(8,128)(2,1)}, bf16[320,12,64]{0,2,1:T(8,128)(2,1)S(1)}, u32[]{:S(2)}) copy-start(bf16[320,12,64]{0,2,1:T(8,128)(2,1)S(1)} %divide_convert_fusion) | copy-start | bytes 1474564
  259.0 82.3 %copy-start.12 = (f32[768]{0:T(1024)S(1)}, f32[768]{0:T(1024)}, u32[]{:S(2)}) copy-start(f32[768]{0:T(1024)} %param.17) | copy-start | bytes 9220
  278.2 128.9 %copy-start.8 = (bf16[320,768]{1,0:T(8,128)(2,1)S(1)}, bf16[320,768]{1,0:T(8,128)(2,1)}, u32[]{:S(2)}) copy-start(bf16[320,768]{1,0:T(8,128)(2,1)} %param.11) | copy-start | bytes 1474564
  407.1 7.8 copy-start.24
  415.0 2.5 copy-start.7
  415.0 2.5 copy-start.21
  415.0 2.9 copy-start.3
  444.1 1.5 copy-start.19
  444.1 171.5 %reduce-scatter.19.cloned.1.call-start = ((), (), s32[]{:S(2)}) async-start(), calls=%async_computation.16 | async-start | bytes 4423680
  491.0 1.1 copy-start.2
  491.0 229.3 %reduce-scatter.13.cloned.1.call-start = ((), (), s32[]{:S(2)}) async-start(), calls=%async_computation.13 | async-start | bytes 2433024 | tf_op jit(solution)/shard_map/reduce_scatter | solution.py:193
  494.3 368.1 %reduce-scatter.15.cloned.1.call-start = ((), (), s32[]{:S(2)}) async-start(), calls=%async_computation.14 | async-start | bytes 9732096 | tf_op jit(solution)/shard_map/reduce_scatter | solution.py:194
  501.2 1.0 copy-start.9
  501.2 1.0 copy-start.22
  501.2 502.1 %reduce-scatter.17.cloned.1.call-start = ((), (), s32[]{:S(2)}) async-start(), calls=%async_computation.15 | async-start | bytes 9732096 | tf_op jit(solution)/shard_map/reduce_scatter | solution.py:195
  511.0 106.7 %copy-start.13 = (f32[768]{0:T(1024)S(1)}, f32[768]{0:T(1024)}, u32[]{:S(2)}) copy-start(f32[768]{0:T(1024)} %param.16) | copy-start | bytes 9220
  511.0 106.7 %copy-start.16 = (f32[320]{0:T(512)S(1)}, f32[320]{0:T(512)}, u32[]{:S(2)}) copy-start(f32[320]{0:T(512)} %copy-done.15) | copy-start | bytes 3844
  511.0 106.7 %copy-start.18 = (f32[320]{0:T(512)S(1)}, f32[320]{0:T(512)}, u32[]{:S(2)}) copy-start(f32[320]{0:T(512)} %copy-done.17) | copy-start | bytes 3844
  511.0 617.7 %reduce-scatter.11.cloned.1.call-start = ((), (), s32[]{:S(2)}) async-start(), calls=%async_computation.12 | async-start | bytes 7299072 | tf_op jit(solution)/shard_map/reduce_scatter | solution.py:192
  624.1 6.9 copy-start.5
  624.1 6.9 copy-start.6
  624.1 6.9 copy-start.25
  631.0 1.9 copy-start.23
Sparse Core Ops, SparseCore 0:
  11.5 62.8 all-gather.6
  79.2 68.8 all-gather.8
  150.9 68.4 all-gather.10
  222.7 52.6 all-gather.12
  278.7 62.5 all-gather.14
  344.6 62.4 all-gather.16
  444.2 83.1 reduce-scatter.20
  531.5 83.9 reduce-scatter.18
  621.4 98.8 reduce-scatter.12
  727.6 134.6 reduce-scatter.14
  868.8 134.4 reduce-scatter.16
  1010.4 118.2 reduce-scatter.10
where the time goes:
time: 1150 us; the launch traced here: 1140 us
  waiting for transfers between devices  860 us (75%)
  matrix products  156 us (14%)
  blocking collectives  40.4 us (4%)
  local copies, waits for them, and re-layouts  35 us (3%)
  other arithmetic  28.3 us (2%)
  between operations  15.4 us (1%)
    reduce_scatter x1, waiting for transfers between devices, on_device(): lax.psum_scatter(up_grad, ('scene', 'seq'), scatter_dimension=0, tiled=True)  142 us
    reduce_scatter x1, waiting for transfers between devices, on_device(): lax.psum_scatter(down_grad, ('scene', 'seq'), scatter_dimension=0, tiled=...  141 us
    reduce_scatter x1, waiting for transfers between devices, on_device(): lax.psum_scatter(qkv_grad, ('scene', 'seq'), scatter_dimension=0, tiled=T...  125 us
    unnamed x14, waiting for transfers between devices  92.4 us
    all_gather x1, waiting for transfers between devices, on_device(): key_piece = lax.all_gather(key_rows, 'seq', axis=0, tiled=True)  65 us
    all_gather x1, waiting for transfers between devices, on_device(): lax.all_gather(up_part, ('scene', 'seq'), axis=0, tiled=True)  63 us
    all_gather x1, waiting for transfers between devices, on_device(): lax.all_gather(qkv_part, ('scene', 'seq'), axis=0, tiled=True)  63 us
    all_gather x1, waiting for transfers between devices, on_device(): lax.all_gather(down_part, ('scene', 'seq'), axis=0, tiled=True)  59.8 us
  transfers between devices with their start and end apart: 12, of which 12 were waited for; matrix products, arithmetic and copies ran while one was open for 15% of the time, Pallas kernels for 0%

commit v1 on v0

--- a/solution.py
+++ b/solution.py
@@ -82,7 +82,12 @@
         return places % local_rows < live_count
 
     row_max = jnp.full((HEADS, local_rows), NEG_BIG, jnp.float32)
-    key_piece = lax.all_gather(key_rows, "seq", axis=0, tiled=True)
+    ring = [key_rows]
+    for hop in range(7):
+        ring.append(lax.ppermute(ring[-1], "seq", [(dev, (dev + 1) % 8) for dev in range(8)]))
+    key_piece = jnp.roll(
+        jnp.concatenate(ring[::-1], axis=0), (lax.axis_index("seq") + 1) * ring[0].shape[0], axis=0
+    )
     value_piece = lax.all_gather(value_rows, "seq", axis=0, tiled=True)
     piece_rows = key_piece.shape[0]
     scores = (

time: 1150 us -> 1230 us (1.070)
  waiting for transfers between devices: 860 us -> 915 us
  matrix products: 156 us -> 173 us
  local copies, waits for them, and re-layouts: 35 us -> 50.7 us
    ppermute x0 -> x7, waiting for transfers between devices: none -> 136 us  [on_device(): lax.ppermute(ring[-1], 'seq', [(dev, (dev + 1) % 8) for dev in range(8)])]
    all_gather x1, waiting for transfers between devices: 65 us -> 0.01 us  [on_device(): key_piece = lax.all_gather(key_rows, 'seq', axis=0, tiled=True)]
    all_gather x1, waiting for transfers between devices: 47.9 us -> 0.01 us  [on_device(): value_piece = lax.all_gather(value_rows, 'seq', axis=0, tiled=True)]
    unnamed x14, waiting for transfers between devices: 92.4 us -> 114 us
    dot_general x0 -> x1, matrix products: none -> 16.8 us  [score_grads(): jnp.einsum('qhd,khd->hqk', query_part, key_part, preferred_element_type=j...]
  transfers between devices with their start and end apart: 12 -> 19, of which waited for: 12 -> 17; matrix products, arithmetic and copies ran while one was open for 15% -> 15% of each run, Pallas kernels for 0% -> 0%
where the time goes in v1:
time: 1230 us
  waiting for transfers between devices  915 us (74%)
  matrix products  173 us (14%)
  local copies, waits for them, and re-layouts  50.7 us (4%)
  blocking collectives  40.4 us (3%)
  other arithmetic  28 us (2%)
  between operations  15.6 us (1%)
    reduce_scatter x1, waiting for transfers between devices, on_device(): lax.psum_scatter(down_grad, ('scene', 'seq'), scatter_dimension=0, tiled=...  142 us
    reduce_scatter x1, waiting for transfers between devices, on_device(): lax.psum_scatter(up_grad, ('scene', 'seq'), scatter_dimension=0, tiled=True)  141 us
    ppermute x7, waiting for transfers between devices, on_device(): lax.ppermute(ring[-1], 'seq', [(dev, (dev + 1) % 8) for dev in range(8)])  136 us
    reduce_scatter x1, waiting for transfers between devices, on_device(): lax.psum_scatter(qkv_grad, ('scene', 'seq'), scatter_dimension=0, tiled=T...  125 us
    unnamed x14, waiting for transfers between devices  114 us
    all_gather x1, waiting for transfers between devices, on_device(): lax.all_gather(up_part, ('scene', 'seq'), axis=0, tiled=True)  63.7 us
    all_gather x1, waiting for transfers between devices, on_device(): lax.all_gather(qkv_part, ('scene', 'seq'), axis=0, tiled=True)  63 us
    all_gather x1, waiting for transfers between devices, on_device(): lax.all_gather(down_part, ('scene', 'seq'), axis=0, tiled=True)  59.9 us
  transfers between devices with their start and end apart: 19, of which 17 were waited for; matrix products, arithmetic and copies ran while one was open for 15% of the time, Pallas kernels for 0%

profile of v1, /device:TPU:0, one launch (start us, length us, event | category | flops | bytes accessed | tf_op | source)
XLA Modules:
  0.0 1226.2 jit_solution(2161179494009830598)
XLA Ops:
  7.2 1.6 convert_element_type.98
  8.9 1.2 convert_reduce_fusion
  10.1 1.3 fusion.37
  11.4 63.0 %all-gather.7.cloned.1.call-done = bf16[768,2304]{1,0:T(8,128)(2,1)} async-done(((bf16[24,2304]{1,0:T(8,128)(2,1)}), bf16[768,2304]{1,0:T(8,128)(2,1)}) %all-gather.7.cloned.1.call-update) | async-done | bytes 3538960 | tf_op jit(solution)/shard_map/all_gather | solution.py:64
  74.4 3.6 convolution_convert_fusion
  78.0 0.8 slice.13
  78.9 1.5 collective-permute-start
  80.4 19.1 %collective-permute-done = bf16[320,768]{1,0:T(8,128)(2,1)S(1)} collective-permute-done((bf16[320,768]{1,0:T(8,128)(2,1)}, bf16[320,768]{1,0:T(8,128)(2,1)S(1)}, u32[]{:S(2)}, u32[]{:S(2)}) %collective-permute-start) | collective-permute-done | bytes 491552 | tf_op jit(solution)/shard_map/ppermute | solution.py:87
  99.5 22.1 %collective-permute-done.1 = bf16[320,768]{1,0:T(8,128)(2,1)S(1)} collective-permute-done((bf16[320,768]{1,0:T(8,128)(2,1)S(1)}, bf16[320,768]{1,0:T(8,128)(2,1)S(1)}, u32[]{:S(2)}, u32[]{:S(2)}) %collective-permute-start.1) | collective-permute-done | bytes 491552 | tf_op jit(solution)/shard_map/ppermute | solution.py:87
  121.6 26.6 %collective-permute-done.2 = bf16[320,768]{1,0:T(8,128)(2,1)S(1)} collective-permute-done((bf16[320,768]{1,0:T(8,128)(2,1)S(1)}, bf16[320,768]{1,0:T(8,128)(2,1)S(1)}, u32[]{:S(2)}, u32[]{:S(2)}) %collective-permute-start.2) | collective-permute-done | bytes 491552 | tf_op jit(solution)/shard_map/ppermute | solution.py:87
  148.2 26.4 %collective-permute-done.3 = bf16[320,768]{1,0:T(8,128)(2,1)S(1)} collective-permute-done((bf16[320,768]{1,0:T(8,128)(2,1)S(1)}, bf16[320,768]{1,0:T(8,128)(2,1)S(1)}, u32[]{:S(2)}, u32[]{:S(2)}) %collective-permute-start.3) | collective-permute-done | bytes 491552 | tf_op jit(solution)/shard_map/ppermute | solution.py:87
  174.6 14.8 %collective-permute-done.4 = bf16[320,768]{1,0:T(8,128)(2,1)S(1)} collective-permute-done((bf16[320,768]{1,0:T(8,128)(2,1)S(1)}, bf16[320,768]{1,0:T(8,128)(2,1)S(1)}, u32[]{:S(2)}, u32[]{:S(2)}) %collective-permute-start.4) | collective-permute-done | bytes 491552 | tf_op jit(solution)/shard_map/ppermute | solution.py:87
  189.5 13.9 %collective-permute-done.5 = bf16[320,768]{1,0:T(8,128)(2,1)S(1)} collective-permute-done((bf16[320,768]{1,0:T(8,128)(2,1)S(1)}, bf16[320,768]{1,0:T(8,128)(2,1)S(1)}, u32[]{:S(2)}, u32[]{:S(2)}) %collective-permute-start.5) | collective-permute-done | bytes 491552 | tf_op jit(solution)/shard_map/ppermute | solution.py:87
  203.4 13.0 %collective-permute-done.6 = bf16[320,768]{1,0:T(8,128)(2,1)S(1)} collective-permute-done((bf16[320,768]{1,0:T(8,128)(2,1)S(1)}, bf16[320,768]{1,0:T(8,128)(2,1)S(1)}, u32[]{:S(2)}, u32[]{:S(2)}) %collective-permute-start.6) | collective-permute-done | bytes 491552 | tf_op jit(solution)/shard_map/ppermute | solution.py:87
  217.0 0.9 constant_dynamic-update-slice_fusion
  217.9 3.0 copy-done.4
  221.0 0.6 convert_element_type.103
  221.8 0.7 convert_element_type.105
  222.5 0.7 convert_element_type.107
  224.5 5.2 constant_dynamic-slice_fusion
  229.7 6.3 copy.31
  236.3 17.5 %fusion = (f32[12,320]{1,0:T(8,128)S(1)}, f32[12,320,2560]{2,1,0:T(8,128)}) fusion(pred[2560]{0:T(1024)(128)(4,1)S(1)} %fusion.52, bf16[320,12,64]{0,2,1:T(8,128)(2,1)S(1)} %bitcast.54, bf16[2560,12,64]{0,2,1:T(8,128)(2,1)} %bitcast.52), kind=kOutput, calls=%fused_computation.4 | convolution fusion | flops 1287778560 | bytes 43763200 | tf_op jit(solution)/shard_map/qhd,khd->hqk/dot_general | solution.py:94
  253.9 17.8 %fusion.1 = f32[12,320]{1,0:T(8,128)S(1)} fusion(f32[12,320,2560]{2,1,0:T(8,128)} %get-tuple-element.20, f32[12,320]{1,0:T(8,128)S(1)} %broadcast_maximum_fusion, pred[2560]{0:T(1024)(128)(4,1)S(1)} %fusion.52), kind=kLoop, calls=%fused_computation.5 | loop fusion | flops 39317760 | bytes 39354880 | tf_op jit(solution)/shard_map/reduce_sum | solution.py:102
  271.7 0.6 log_add_fusion
  272.3 6.2 copy.33
  278.5 16.8 %fusion.68 = f32[12,320,2560]{2,1,0:T(8,128)} fusion(bf16[320,12,64]{0,2,1:T(8,128)(2,1)S(1)} %bitcast.55, bf16[2560,12,64]{0,2,1:T(8,128)(2,1)} %bitcast.50), kind=kOutput, calls=%fused_computation.111 | convolution fusion | flops 1258291200 | bytes 43745280 | tf_op jit(solution)/shard_map/qhd,khd->hqk/dot_general | solution.py:34
  295.3 6.3 copy.32
  301.6 16.4 %divide_convert_fusion = bf16[320,12,64]{0,2,1:T(8,128)(2,1)S(1)} fusion(bf16[2560,12,64]{0,2,1:T(8,128)(2,1)} %bitcast.59, f32[12,320,2560]{2,1,0:T(8,128)} %get-tuple-element.20, f32[12,320]{1,0:T(8,128)S(1)} %broadcast_maximum_fusion, pred[2560]{0:T(1024)(128)(4,1)S(1)} %fusion.52, f32[320,12]{0,1:T(8,128)S(1)} %bitcast.67), kind=kOutput, calls=%fused_computation.36 | convolution fusion | flops 1298104320 | bytes 43778560 | tf_op jit(solution)/shard_map/hqk,khd->hqd/dot_general | solution.py:103
  318.0 26.5 %all-gather.11.cloned.1.call-done = bf16[768,768]{1,0:T(8,128)(2,1)} async-done(((bf16[24,768]{1,0:T(8,128)(2,1)}), bf16[768,768]{1,0:T(8,128)(2,1)}) %all-gather.11.cloned.1.call-update) | async-done | bytes 1179664 | tf_op jit(solution)/shard_map/all_gather | solution.py:65
  344.6 1.9 fusion.67
  346.8 63.7 %all-gather.13.cloned.1.call-done = bf16[768,3072]{1,0:T(8,128)(2,1)} async-done(((bf16[24,3072]{1,0:T(8,128)(2,1)}), bf16[768,3072]{1,0:T(8,128)(2,1)}) %all-gather.13.cloned.1.call-update) | async-done | bytes 4718608 | tf_op jit(solution)/shard_map/all_gather | solution.py:66
  410.5 6.0 fusion.66
  416.4 59.9 %all-gather.15.cloned.1.call-done = bf16[3072,768]{1,0:T(8,128)(2,1)} async-done(((bf16[96,768]{1,0:T(8,128)(2,1)}), bf16[3072,768]{1,0:T(8,128)(2,1)}) %all-gather.15.cloned.1.call-update) | async-done | bytes 4718608 | tf_op jit(solution)/shard_map/all_gather | solution.py:67
  476.3 7.4 fusion.19
  483.7 2.5 multiply_reduce_fusion.1
  486.6 0.6 convolution_convert_fusion.1
  487.2 1.1 copy.34
  488.3 1.4 multiply_reduce_fusion
  489.7 26.1 %multiply_convert_fusion = bf16[12,320,2560]{2,1,0:T(8,128)(2,1)} fusion(f32[12,320,2560]{2,1,0:T(8,128)} %fusion.68, bf16[320,12,64]{0,2,1:T(8,128)(2,1)} %bitcast.65, bf16[2560,12,64]{0,2,1:T(8,128)(2,1)} %bitcast.60, f32[12,320]{1,0:T(8,128)S(1)} %bitcast.68, f32[12,320]{1,0:T(8,128)} %log_add_fusion, pred[2560]{0:T(1024)(128)(4,1)S(1)} %fusion.52), kind=kOutput, calls=%fused_computation | convolution fusion | flops 1317273600 | bytes 63439360 | tf_op jit(solution)/shard_map/qhd,khd->hqk/dot_general | solution.py:37
  515.8 12.4 %multiply_convert_fusion.1 = bf16[12,64,2560]{2,1,0:T(8,128)(2,1)} fusion(bf16[320,12,64]{0,2,1:T(8,128)(2,1)S(1)} %bitcast.56, bf16[12,320,2560]{2,1,0:T(8,128)(2,1)} %multiply_convert_fusion), kind=kOutput, calls=%fused_computation.12 | convolution fusion | flops 1262223360 | bytes 24084480 | tf_op jit(solution)/shard_map/hqk,qhd->khd/dot_general | solution.py:165
  528.2 6.3 copy.35
  534.6 1.0 copy-done.7
  535.6 18.3 %fusion.10 = bf16[12,64,2560]{2,1,0:T(8,128)(2,1)} fusion(bf16[320,12,64]{0,2,1:T(8,128)(2,1)S(1)} %bitcast.66, f32[12,320,2560]{2,1,0:T(8,128)} %fusion.68, f32[12,320]{1,0:T(8,128)S(1)} %copy-done.20, pred[2560]{0:T(1024)(128)(4,1)S(1)} %fusion.52), kind=kOutput, calls=%fused_computation.15 | convolution fusion | flops 1299578880 | bytes 43763200 | tf_op jit(solution)/shard_map/hqk,qhd->khd/dot_general | solution.py:167
  553.8 6.3 copy.37
  560.3 1.0 copy-done.2
  561.3 2.2 fusion.43
  563.5 8.8 fusion.46
  572.4 6.8 fusion.65
  579.3 11.1 fusion.24
  590.4 27.4 %reduce-scatter.19.cloned.1.call-done = bf16[320,768]{1,0:T(8,128)(2,1)} async-done(((bf16[2560,768]{1,0:T(8,128)(2,1)}), bf16[320,768]{1,0:T(8,128)(2,1)}) %reduce-scatter.19.cloned.1.call-update) | async-done | bytes 491536
  617.8 2.1 copy.36
  619.9 86.1 %reduce-scatter.21.cloned.1.call-done = bf16[320,768]{1,0:T(8,128)(2,1)} async-done(((bf16[2560,768]{1,0:T(8,128)(2,1)}), bf16[320,768]{1,0:T(8,128)(2,1)}) %reduce-scatter.21.cloned.1.call-update) | async-done | bytes 491536
  706.0 2.1 copy.38
  708.1 6.4 fusion.39
  714.5 6.9 fusion.23
  721.5 1.9 fusion.36
  723.4 40.4 %all-reduce.2 = (f32[768]{0:T(1024)S(1)}, f32[768]{0:T(1024)S(1)}) all-reduce(f32[768]{0:T(1024)S(1)} %get-tuple-element.10, f32[768]{0:T(1024)S(1)} %copy-done.24), channel_id=8, replica_groups=mesh['scene'=4,'seq'=8] {'scene','seq'}, use_global_device_ids=true, to_apply=%region_18.19.clone | all-reduce | flops 1536 | bytes 12288
  763.8 0.6 dynamic-slice
  764.3 0.6 dynamic-slice.1
  764.9 1.3 fusion.35
  766.2 44.5 %reduce-scatter.13.cloned.1.call-done = f32[24,768]{1,0:T(8,128)} async-done(((f32[768,768]{1,0:T(8,128)}), f32[24,768]{1,0:T(8,128)}) %reduce-scatter.13.cloned.1.call-update) | async-done | bytes 73744 | tf_op jit(solution)/shard_map/reduce_scatter | solution.py:198
  810.8 141.8 %reduce-scatter.17.cloned.1.call-done = f32[96,768]{1,0:T(8,128)} async-done(((f32[3072,768]{1,0:T(8,128)}), f32[96,768]{1,0:T(8,128)}) %reduce-scatter.17.cloned.1.call-update) | async-done | bytes 294928 | tf_op jit(solution)/shard_map/reduce_scatter | solution.py:200
  952.5 141.1 %reduce-scatter.15.cloned.1.call-done = f32[24,3072]{1,0:T(8,128)} async-done(((f32[768,3072]{1,0:T(8,128)}), f32[24,3072]{1,0:T(8,128)}) %reduce-scatter.15.cloned.1.call-update) | async-done | bytes 294928 | tf_op jit(solution)/shard_map/reduce_scatter | solution.py:199
  1093.7 125.4 %reduce-scatter.11.cloned.1.call-done = f32[24,2304]{1,0:T(8,128)} async-done(((f32[768,2304]{1,0:T(8,128)}), f32[24,2304]{1,0:T(8,128)}) %reduce-scatter.11.cloned.1.call-update) | async-done | bytes 221200 | tf_op jit(solution)/shard_map/reduce_scatter | solution.py:197
  (111 shorter events, 2.9 us)
Async XLA Ops:
  7.2 67.2 %all-gather.7.cloned.1.call-start = ((), (), s32[]{:S(2)}) async-start(), calls=%async_computation.6 | async-start | bytes 3649536 | tf_op jit(solution)/shard_map/all_gather | solution.py:64
  8.8 263.5 %all-gather.17.cloned.1.call-start = ((), (), s32[]{:S(2)}) async-start(), calls=%async_computation.11 | async-start | bytes 4423680 | tf_op jit(solution)/shard_map/all_gather | solution.py:148
  10.1 67.9 %copy-start.16 = (f32[320]{0:T(512)}, f32[320]{0:T(512)S(1)}, u32[]{:S(2)}) copy-start(f32[320]{0:T(512)S(1)} %broadcast_multiply_fusion.5) | copy-start | bytes 3844
  11.4 66.6 %copy-start.18 = (f32[320]{0:T(512)}, f32[320]{0:T(512)S(1)}, u32[]{:S(2)}) copy-start(f32[320]{0:T(512)S(1)} %add_rsqrt_fusion.1) | copy-start | bytes 3844
  78.8 216.5 %all-gather.9.cloned.1.call-start = ((), (), s32[]{:S(2)}) async-start(), calls=%async_computation.7 | async-start | bytes 4423680 | tf_op jit(solution)/shard_map/all_gather | solution.py:91
  78.9 20.6 %collective-permute-start = (bf16[320,768]{1,0:T(8,128)(2,1)}, bf16[320,768]{1,0:T(8,128)(2,1)S(1)}, u32[]{:S(2)}, u32[]{:S(2)}) collective-permute-start(bf16[320,768]{1,0:T(8,128)(2,1)} %slice.13), channel_id=1, source_target_pairs={{0,1},{1,2},{2,3},{3,4},{4,5},{5,6},{6,7},{7,0},{8,9},{9,10},{10,1... | collective-permute-start | bytes 1474568 | tf_op jit(solution)/shard_map/ppermute | solution.py:87
  99.5 22.1 %collective-permute-start.1 = (bf16[320,768]{1,0:T(8,128)(2,1)S(1)}, bf16[320,768]{1,0:T(8,128)(2,1)S(1)}, u32[]{:S(2)}, u32[]{:S(2)}) collective-permute-start(bf16[320,768]{1,0:T(8,128)(2,1)S(1)} %collective-permute-done), channel_id=1, source_target_pairs={{0,1},{1,2},{2,3},{3,4},{4,5},{5,6},{6,7},{7,0},{8,9},{9,10},{10,1... | collective-permute-start | bytes 1474568 | tf_op jit(solution)/shard_map/ppermute | solution.py:87
  121.6 26.6 %collective-permute-start.2 = (bf16[320,768]{1,0:T(8,128)(2,1)S(1)}, bf16[320,768]{1,0:T(8,128)(2,1)S(1)}, u32[]{:S(2)}, u32[]{:S(2)}) collective-permute-start(bf16[320,768]{1,0:T(8,128)(2,1)S(1)} %collective-permute-done.1), channel_id=1, source_target_pairs={{0,1},{1,2},{2,3},{3,4},{4,5},{5,6},{6,7},{7,0},{8,9},{9,10},{10,1... | collective-permute-start | bytes 1474568 | tf_op jit(solution)/shard_map/ppermute | solution.py:87
  148.2 26.4 %collective-permute-start.3 = (bf16[320,768]{1,0:T(8,128)(2,1)S(1)}, bf16[320,768]{1,0:T(8,128)(2,1)S(1)}, u32[]{:S(2)}, u32[]{:S(2)}) collective-permute-start(bf16[320,768]{1,0:T(8,128)(2,1)S(1)} %collective-permute-done.2), channel_id=1, source_target_pairs={{0,1},{1,2},{2,3},{3,4},{4,5},{5,6},{6,7},{7,0},{8,9},{9,10},{10,1... | collective-permute-start | bytes 1474568 | tf_op jit(solution)/shard_map/ppermute | solution.py:87
  174.6 14.8 %collective-permute-start.4 = (bf16[320,768]{1,0:T(8,128)(2,1)S(1)}, bf16[320,768]{1,0:T(8,128)(2,1)S(1)}, u32[]{:S(2)}, u32[]{:S(2)}) collective-permute-start(bf16[320,768]{1,0:T(8,128)(2,1)S(1)} %collective-permute-done.3), channel_id=1, source_target_pairs={{0,1},{1,2},{2,3},{3,4},{4,5},{5,6},{6,7},{7,0},{8,9},{9,10},{10,1... | collective-permute-start | bytes 1474568 | tf_op jit(solution)/shard_map/ppermute | solution.py:87
  189.5 13.9 %collective-permute-start.5 = (bf16[320,768]{1,0:T(8,128)(2,1)S(1)}, bf16[320,768]{1,0:T(8,128)(2,1)S(1)}, u32[]{:S(2)}, u32[]{:S(2)}) collective-permute-start(bf16[320,768]{1,0:T(8,128)(2,1)S(1)} %collective-permute-done.4), channel_id=1, source_target_pairs={{0,1},{1,2},{2,3},{3,4},{4,5},{5,6},{6,7},{7,0},{8,9},{9,10},{10,1... | collective-permute-start | bytes 1474568 | tf_op jit(solution)/shard_map/ppermute | solution.py:87
  203.4 13.0 %collective-permute-start.6 = (bf16[320,768]{1,0:T(8,128)(2,1)S(1)}, bf16[320,768]{1,0:T(8,128)(2,1)S(1)}, u32[]{:S(2)}, u32[]{:S(2)}) collective-permute-start(bf16[320,768]{1,0:T(8,128)(2,1)S(1)} %collective-permute-done.5), channel_id=1, source_target_pairs={{0,1},{1,2},{2,3},{3,4},{4,5},{5,6},{6,7},{7,0},{8,9},{9,10},{10,1... | collective-permute-start | bytes 1474568 | tf_op jit(solution)/shard_map/ppermute | solution.py:87
  216.8 4.2 copy-start.15
  216.9 4.9 copy-start.11
  216.9 5.6 copy-start.12
  217.9 3.0 copy-start.4
  221.0 123.6 %all-gather.11.cloned.1.call-start = ((), (), s32[]{:S(2)}) async-start(), calls=%async_computation.8 | async-start | bytes 1216512 | tf_op jit(solution)/shard_map/all_gather | solution.py:65
  221.7 188.8 %all-gather.13.cloned.1.call-start = ((), (), s32[]{:S(2)}) async-start(), calls=%async_computation.9 | async-start | bytes 4866048 | tf_op jit(solution)/shard_map/all_gather | solution.py:66
  222.5 253.9 %all-gather.15.cloned.1.call-start = ((), (), s32[]{:S(2)}) async-start(), calls=%async_computation.10 | async-start | bytes 4866048 | tf_op jit(solution)/shard_map/all_gather | solution.py:67
  223.2 394.6 %reduce-scatter.19.cloned.1.call-start = ((), (), s32[]{:S(2)}) async-start(), calls=%async_computation.16 | async-start | bytes 4423680
  224.5 251.8 %copy-start.21 = (f32[320]{0:T(512)}, f32[320]{0:T(512)S(1)}, u32[]{:S(2)}) copy-start(f32[320]{0:T(512)S(1)} %fusion.56) | copy-start | bytes 3844
  301.6 42.9 %copy-start = (bf16[320,768]{1,0:T(8,128)(2,1)S(1)}, bf16[320,768]{1,0:T(8,128)(2,1)}, u32[]{:S(2)}) copy-start(bf16[320,768]{1,0:T(8,128)(2,1)} %param.9) | copy-start | bytes 1474564
  318.0 98.4 %copy-start.1 = (bf16[320,12,64]{0,2,1:T(8,128)(2,1)}, bf16[320,12,64]{0,2,1:T(8,128)(2,1)S(1)}, u32[]{:S(2)}) copy-start(bf16[320,12,64]{0,2,1:T(8,128)(2,1)S(1)} %divide_convert_fusion) | copy-start | bytes 1474564
  318.0 92.4 %copy-start.13 = (f32[768]{0:T(1024)S(1)}, f32[768]{0:T(1024)}, u32[]{:S(2)}) copy-start(f32[768]{0:T(1024)} %param.17) | copy-start | bytes 9220
  346.8 129.5 %copy-start.9 = (bf16[320,768]{1,0:T(8,128)(2,1)S(1)}, bf16[320,768]{1,0:T(8,128)(2,1)}, u32[]{:S(2)}) copy-start(bf16[320,768]{1,0:T(8,128)(2,1)} %param.11) | copy-start | bytes 1474564
  476.3 7.4 copy-start.25
  483.7 2.5 copy-start.8
  483.7 2.5 copy-start.22
  483.7 2.9 copy-start.3
  534.5 1.1 copy-start.7
  534.5 1.1 copy-start.20
  534.5 171.5 %reduce-scatter.21.cloned.1.call-start = ((), (), s32[]{:S(2)}) async-start(), calls=%async_computation.17 | async-start | bytes 4423680
  560.2 1.1 copy-start.2
  560.2 3.3 copy-start.10
  560.2 3.3 copy-start.23
  560.2 250.5 %reduce-scatter.13.cloned.1.call-start = ((), (), s32[]{:S(2)}) async-start(), calls=%async_computation.13 | async-start | bytes 2433024 | tf_op jit(solution)/shard_map/reduce_scatter | solution.py:198
  563.5 389.1 %reduce-scatter.17.cloned.1.call-start = ((), (), s32[]{:S(2)}) async-start(), calls=%async_computation.15 | async-start | bytes 9732096 | tf_op jit(solution)/shard_map/reduce_scatter | solution.py:200
  572.3 521.3 %reduce-scatter.15.cloned.1.call-start = ((), (), s32[]{:S(2)}) async-start(), calls=%async_computation.14 | async-start | bytes 9732096 | tf_op jit(solution)/shard_map/reduce_scatter | solution.py:199
  579.2 128.8 %copy-start.14 = (f32[768]{0:T(1024)S(1)}, f32[768]{0:T(1024)}, u32[]{:S(2)}) copy-start(f32[768]{0:T(1024)} %param.16) | copy-start | bytes 9220
  579.2 128.8 %copy-start.17 = (f32[320]{0:T(512)S(1)}, f32[320]{0:T(512)}, u32[]{:S(2)}) copy-start(f32[320]{0:T(512)} %copy-done.16) | copy-start | bytes 3844
  579.3 128.8 %copy-start.19 = (f32[320]{0:T(512)S(1)}, f32[320]{0:T(512)}, u32[]{:S(2)}) copy-start(f32[320]{0:T(512)} %copy-done.18) | copy-start | bytes 3844
  579.3 639.8 %reduce-scatter.11.cloned.1.call-start = ((), (), s32[]{:S(2)}) async-start(), calls=%async_computation.12 | async-start | bytes 7299072 | tf_op jit(solution)/shard_map/reduce_scatter | solution.py:197
  714.5 6.9 copy-start.5
  714.5 6.9 copy-start.6
  714.5 6.9 copy-start.26
  721.4 1.9 copy-start.24
Sparse Core Ops, SparseCore 0:
  11.5 62.8 all-gather.6
  78.9 95.1 all-gather.16
  221.1 67.4 all-gather.8
  292.0 52.5 all-gather.10
  347.9 62.5 all-gather.12
  413.8 62.4 all-gather.14
  534.6 83.1 reduce-scatter.18
  622.0 83.9 reduce-scatter.20
  711.9 98.8 reduce-scatter.12
  818.1 134.3 reduce-scatter.16
  959.0 134.6 reduce-scatter.14
  1100.7 118.2 reduce-scatter.10
